TPU v7x, 256 devices: a whole 4x4x8 slice. The times are simulated.
256 devices in a mesh: row: 32 (over z, y), col: 8 (over x, core).
Axes of the slice: x: 4, y: 4, z: 8, core: 2. Of those that a mesh axis runs over, the one named last changes fastest.
Arguments:
- covariance: float32 [16384, 16384], P('row', 'col'), as said below
- courant: float32 [2, 16384], replicated, may hold values from 0.05 to 0.45
- upwind: int32 [16384], replicated, may hold values from 0 to 3
- observed: int32 [2, 256], replicated, may hold values from 0 to 16383
- noise: float32 [2, 256], replicated, may hold values from 0.5 to 2
Outputs:
- posterior: float32 [16384, 16384], P('row', 'col')
Inputs may be any that keep to these rules, and one draw needn't show every extreme that they name: The covariance is symmetric and positive definite.
All inputs are finite; a program needn't handle non-finite values.
Results may differ from a plain program's by a relative error of at most 0.0003.
Values sent between devices are 32-bit elements; how exact they have to be, the bound alone decides.
No kernel may reach another device: no remote copies, remote signals or barrier semaphores. Data moves between devices by JAX's collectives and lax.ppermute only.
A program may use at most 64 MiB of HBM per device.

v0:
```python
import jax
import jax.numpy as jnp
from jax import lax
from jax.sharding import PartitionSpec as P

G = 128
BATCHES = 2


def extended(block, sides, width):
    for axis, dim in sides:
        count = lax.axis_size(axis)
        forward = [(i, i + 1) for i in range(count - 1)]
        backward = [(target, source) for source, target in forward]
        low = lax.ppermute(
            lax.slice_in_dim(block, block.shape[dim] - width, None, axis=dim), axis, forward
        )
        high = lax.ppermute(lax.slice_in_dim(block, 0, width, axis=dim), axis, backward)
        block = jnp.concatenate([low, block, high], axis=dim)
    return block


def left_apply(padded, cour_a, cour_b, up_dir):
    lines = padded.shape[0] - 2
    center = padded[1:-1]
    prev_line = padded[:-2]
    next_line = padded[2:]
    prev_cell = jnp.pad(center, ((0, 0), (1, 0), (0, 0)))[:, :-1]
    next_cell = jnp.pad(center, ((0, 0), (0, 1), (0, 0)))[:, 1:]
    coef_a = cour_a.reshape(lines, G, 1)
    coef_b = cour_b.reshape(lines, G, 1)
    dirs = up_dir.reshape(lines, G, 1)
    up_line = jnp.where(dirs % 2 == 1, next_line, prev_line)
    up_cell = jnp.where(dirs // 2 == 1, next_cell, prev_cell)
    return (1.0 - coef_a - coef_b) * center + coef_a * up_line + coef_b * up_cell


def right_apply(padded, cour_a, cour_b, up_dir):
    lines = padded.shape[1] - 2
    center = padded[:, 1:-1]
    prev_line = padded[:, :-2]
    next_line = padded[:, 2:]
    prev_cell = jnp.pad(center, ((0, 0), (0, 0), (1, 0)))[:, :, :-1]
    next_cell = jnp.pad(center, ((0, 0), (0, 0), (0, 1)))[:, :, 1:]
    coef_a = cour_a.reshape(1, lines, G)
    coef_b = cour_b.reshape(1, lines, G)
    dirs = up_dir.reshape(1, lines, G)
    up_line = jnp.where(dirs % 2 == 1, next_line, prev_line)
    up_cell = jnp.where(dirs // 2 == 1, next_cell, prev_cell)
    return (1.0 - coef_a - coef_b) * center + coef_a * up_line + coef_b * up_cell


def transport(block, row_cour, row_dirs, col_cour, col_dirs):
    row_count, col_count = block.shape
    padded = extended(block, (("row", 0),), G)
    padded = padded.reshape(row_count // G + 2, G, col_count)
    block = left_apply(padded, row_cour[0], row_cour[1], row_dirs).reshape(row_count, col_count)
    padded = extended(block, (("col", 1),), G)
    padded = padded.reshape(row_count, col_count // G + 2, G)
    return right_apply(padded, col_cour[0], col_cour[1], col_dirs).reshape(row_count, col_count)


def shards(covariance, courant, upwind, observed, noise):
    row_count, col_count = covariance.shape
    row_start = lax.axis_index("row") * row_count
    col_start = lax.axis_index("col") * col_count
    row_cour = lax.dynamic_slice_in_dim(courant, row_start, row_count, 1)
    col_cour = lax.dynamic_slice_in_dim(courant, col_start, col_count, 1)
    row_dirs = lax.dynamic_slice_in_dim(upwind, row_start, row_count, 0)
    col_dirs = lax.dynamic_slice_in_dim(upwind, col_start, col_count, 0)
    block = covariance
    for cycle in range(BATCHES):
        block = transport(block, row_cour, row_dirs, col_cour, col_dirs)
        obs = observed[cycle]
        local_rows = obs - row_start
        owns_row = (local_rows >= 0) & (local_rows < row_count)
        row_pick = jnp.clip(local_rows, 0, row_count - 1)
        local_cols = obs - col_start
        owns_col = (local_cols >= 0) & (local_cols < col_count)
        col_pick = jnp.clip(local_cols, 0, col_count - 1)
        row_part = jnp.where(owns_row[:, None], jnp.take(block, row_pick, axis=0), 0.0)
        col_part = jnp.where(owns_col[None, :], jnp.take(block, col_pick, axis=1), 0.0)
        row_panel = lax.psum(row_part, "row")
        block_part = jnp.where(owns_col[None, :], jnp.take(row_panel, col_pick, axis=1), 0.0)
        col_panel, innov = lax.psum((col_part, block_part), "col")
        innov = innov + jnp.diag(noise[cycle])
        factor = jnp.linalg.cholesky(innov)
        gain = jax.scipy.linalg.cho_solve((factor, True), col_panel.T).T
        block = block - jnp.dot(
            gain, row_panel, precision=lax.Precision.HIGHEST, preferred_element_type=jnp.float32
        )
    return block


def solution(mesh):
    in_specs = (P("row", "col"), P(), P(), P(), P())
    out_specs = P("row", "col")
    return jax.shard_map(shards, mesh=mesh, in_specs=in_specs, out_specs=out_specs, check_vma=False)
```

profile of v0, /device:TPU:8, one launch (start us, length us, event | category | flops | bytes accessed | tf_op | source)
XLA Modules:
  0.0 755.2 jit_solution(8258046197964841338)
XLA Ops:
  9.2 4.1 collective-permute-start
  19.3 17.0 %collective-permute-done = f32[128,2048]{1,0:T(8,128)S(1)} collective-permute-done((f32[128,2048]{1,0:T(8,128)}, f32[128,2048]{1,0:T(8,128)S(1)}, u32[]{:S(2)}, u32[]{:S(2)}) %collective-permute-start) | collective-permute-done | bytes 1048608 | tf_op jit(solution)/shard_map/ppermute | solution.py:18
  38.1 3.8 pad_maximum_fusion.4
  45.2 5.3 copy.22
  54.2 4.0 collective-permute-done.3
  61.4 3.7 fusion.5
  65.1 5.4 copy.23
  70.5 4.6 gather_fusion
  76.9 3.4 gather_fusion.2
  81.2 158.6 %all-reduce.16.cloned.1.call-done = f32[256,2048]{1,0:T(8,128)} async-done(((f32[256,2048]{1,0:T(8,128)}), f32[256,2048]{1,0:T(8,128)}) %all-reduce.16.cloned.1.call-update) | async-done | bytes 2097168 | tf_op jit(solution)/shard_map/psum | solution.py:83
  243.9 65.5 %all-reduce.22.cloned.1.call-done = (f32[256,512]{1,0:T(8,128)}, f32[256,256]{0,1:T(8,128)}) async-done(((f32[256,512]{1,0:T(8,128)}, f32[256,256]{0,1:T(8,128)}), (f32[256,512]{1,0:T(8,128)}, f32[256,256]{0,1:T(8,128)})) %all-reduce.22.cloned.1.call-update) | async-done | bytes 786448 | tf_op jit(solution)/shard_map/psum | solution.py:85
  311.7 11.7 %cholesky.130 = f32[128,128]{1,0:T(8,128)S(1)} custom-call(f32[128,128]{1,0:T(8,128)S(1)} %cholesky.194), custom_call_target="Cholesky" | custom-call | tf_op jit(solution)/shard_map/jit(cholesky)/cholesky | solution.py:87
  323.5 9.8 %custom-call.15 = f32[1,128,128]{1,2,0:T(8,128)S(1)} custom-call(f32[1,128,128]{2,1,0:T(8,128)S(1)} %get-tuple-element.79), custom_call_target="InvertDiagBlocksLowerTriangular" | custom-call | tf_op jit(solution)/shard_map/jit(cholesky)/cholesky | solution.py:87
  333.8 11.7 %cholesky.147 = f32[128,128]{1,0:T(8,128)S(1)} custom-call(f32[128,128]{1,0:T(8,128)S(1)} %convolution_subtract_fusion.7), custom_call_target="Cholesky" | custom-call | tf_op jit(solution)/shard_map/jit(cholesky)/cholesky | solution.py:87
  348.2 4.1 while.4
  352.4 19.7 %custom-call.16 = f32[2,128,128]{1,2,0:T(8,128)S(1)} custom-call(f32[2,128,128]{2,1,0:T(8,128)S(1)} %get-tuple-element.24), custom_call_target="InvertDiagBlocksLowerTriangular" | custom-call | tf_op jit(solution)/shard_map/jit(_cho_solve)/triangular_solve | solution.py:88
  374.5 5.3 convolution_subtract_fusion.1
  382.5 3.4 collective-permute-start.5
  385.9 18.9 %collective-permute-done.4 = f32[128,2048]{1,0:T(8,128)S(1)} collective-permute-done((f32[128,2048]{1,0:T(8,128)S(1)}, f32[128,2048]{1,0:T(8,128)S(1)}, u32[]{:S(2)}, u32[]{:S(2)}) %collective-permute-start.4) | collective-permute-done | bytes 1048608 | tf_op jit(solution)/shard_map/ppermute | solution.py:18
  413.0 5.3 copy.24
  427.4 3.7 fusion.11
  431.1 5.4 copy.25
  436.5 4.6 gather_fusion.3
  442.8 3.4 gather_fusion.5
  447.2 159.6 %all-reduce.18.cloned.1.call-done = f32[256,2048]{1,0:T(8,128)} async-done(((f32[256,2048]{1,0:T(8,128)}), f32[256,2048]{1,0:T(8,128)}) %all-reduce.18.cloned.1.call-update) | async-done | bytes 2097168 | tf_op jit(solution)/shard_map/psum | solution.py:83
  611.0 65.8 %all-reduce.20.cloned.1.call-done = (f32[256,512]{1,0:T(8,128)}, f32[256,256]{0,1:T(8,128)}) async-done(((f32[256,512]{1,0:T(8,128)}, f32[256,256]{0,1:T(8,128)}), (f32[256,512]{1,0:T(8,128)}, f32[256,256]{0,1:T(8,128)})) %all-reduce.20.cloned.1.call-update) | async-done | bytes 786448 | tf_op jit(solution)/shard_map/psum | solution.py:85
  679.1 11.7 %cholesky.164 = f32[128,128]{1,0:T(8,128)S(1)} custom-call(f32[128,128]{1,0:T(8,128)S(1)} %cholesky.197), custom_call_target="Cholesky" | custom-call | tf_op jit(solution)/shard_map/jit(cholesky)/cholesky | solution.py:87
  690.9 9.8 %custom-call.17 = f32[1,128,128]{1,2,0:T(8,128)S(1)} custom-call(f32[1,128,128]{2,1,0:T(8,128)S(1)} %get-tuple-element.75), custom_call_target="InvertDiagBlocksLowerTriangular" | custom-call | tf_op jit(solution)/shard_map/jit(cholesky)/cholesky | solution.py:87
  701.2 11.7 %cholesky.181 = f32[128,128]{1,0:T(8,128)S(1)} custom-call(f32[128,128]{1,0:T(8,128)S(1)} %convolution_subtract_fusion.6), custom_call_target="Cholesky" | custom-call | tf_op jit(solution)/shard_map/jit(cholesky)/cholesky | solution.py:87
  715.5 3.9 while.5
  719.5 19.8 %custom-call.18 = f32[2,128,128]{1,2,0:T(8,128)S(1)} custom-call(f32[2,128,128]{2,1,0:T(8,128)S(1)} %get-tuple-element.25), custom_call_target="InvertDiagBlocksLowerTriangular" | custom-call | tf_op jit(solution)/shard_map/jit(_cho_solve)/triangular_solve | solution.py:88
  741.8 6.7 convolution_subtract_fusion
  (126 shorter events, 74.8 us)
Async XLA Ops:
  6.5 8.7 %copy-start.5 = (s32[2,256]{1,0:T(2,128)S(1)}, s32[2,256]{1,0:T(2,128)}, u32[]{:S(2)}) copy-start(s32[2,256]{1,0:T(2,128)} %param.17) | copy-start | bytes 6148
  6.5 233.3 %all-reduce.16.cloned.1.call-start = ((), (), s32[]{:S(2)}) async-start(), calls=%async_computation | async-start | bytes 4194304 | tf_op jit(solution)/shard_map/psum | solution.py:83
  9.2 27.0 %collective-permute-start = (f32[128,2048]{1,0:T(8,128)}, f32[128,2048]{1,0:T(8,128)S(1)}, u32[]{:S(2)}, u32[]{:S(2)}) collective-permute-start(f32[128,2048]{1,0:T(8,128)} %get-tuple-element.67), channel_id=1, source_target_pairs={{8,0},{16,8},{24,16},{32,24},{40,32},{48,40},{56,48},{64,56},{72,6... | collective-permute-start | bytes 3145736 | tf_op jit(solution)/shard_map/ppermute | solution.py:18
  13.3 24.8 %collective-permute-start.1 = (f32[128,2048]{1,0:T(8,128)S(1)}, f32[128,2048]{1,0:T(8,128)}, u32[]{:S(2)}, u32[]{:S(2)}) collective-permute-start(f32[128,2048]{1,0:T(8,128)S(1)} %get-tuple-element.66), channel_id=1, source_target_pairs={{0,8},{8,16},{16,24},{24,32},{32,40},{40,48},{48,56},{56,64},{64,7... | collective-permute-start | bytes 3145736 | tf_op jit(solution)/shard_map/ppermute | solution.py:15
  19.3 22.6 %copy-start = (f32[512,2048]{1,0:T(8,128)S(1)}, f32[512,2048]{1,0:T(8,128)}, u32[]{:S(2)}) copy-start(f32[512,2048]{1,0:T(8,128)} %param.14) | copy-start | bytes 12582916
  51.6 2.6 collective-permute-start.2
  52.9 5.3 collective-permute-start.3
  76.8 232.6 %all-reduce.22.cloned.1.call-start = ((), (), s32[]{:S(2)}) async-start(), calls=%async_computation.3 | async-start | bytes 1572864 | tf_op jit(solution)/shard_map/psum | solution.py:85
  81.2 162.7 %copy-start.6 = (f32[2,256]{1,0:T(2,128)S(1)}, f32[2,256]{1,0:T(2,128)}, u32[]{:S(2)}) copy-start(f32[2,256]{1,0:T(2,128)} %param.18) | copy-start | bytes 6148
  243.6 363.2 %all-reduce.18.cloned.1.call-start = ((), (), s32[]{:S(2)}) async-start(), calls=%async_computation.1 | async-start | bytes 4194304 | tf_op jit(solution)/shard_map/psum | solution.py:83
  309.4 62.7 %copy-start.3 = (f32[256,512]{1,0:T(8,128)S(1)}, f32[256,512]{1,0:T(8,128)}, u32[]{:S(2)}) copy-start(f32[256,512]{1,0:T(8,128)} %get-tuple-element.48) | copy-start | bytes 1572868
  310.4 64.0 %copy-start.1 = (f32[256,2048]{1,0:T(8,128)S(1)}, f32[256,2048]{1,0:T(8,128)}, u32[]{:S(2)}) copy-start(f32[256,2048]{1,0:T(8,128)} %all-reduce.16.cloned.1.call-done) | copy-start | bytes 6291460
  380.0 24.8 %collective-permute-start.4 = (f32[128,2048]{1,0:T(8,128)S(1)}, f32[128,2048]{1,0:T(8,128)S(1)}, u32[]{:S(2)}, u32[]{:S(2)}) collective-permute-start(f32[128,2048]{1,0:T(8,128)S(1)} %get-tuple-element.61), channel_id=1, source_target_pairs={{8,0},{16,8},{24,16},{32,24},{40,32},{48,40},{56,48},{64,56},{72,6... | collective-permute-start | bytes 3145736 | tf_op jit(solution)/shard_map/ppermute | solution.py:18
  382.5 24.6 %collective-permute-start.5 = (f32[128,2048]{1,0:T(8,128)S(1)}, f32[128,2048]{1,0:T(8,128)}, u32[]{:S(2)}, u32[]{:S(2)}) collective-permute-start(f32[128,2048]{1,0:T(8,128)S(1)} %get-tuple-element.60), channel_id=1, source_target_pairs={{0,8},{8,16},{16,24},{24,32},{32,40},{40,48},{48,56},{56,64},{64,7... | collective-permute-start | bytes 3145736 | tf_op jit(solution)/shard_map/ppermute | solution.py:15
  419.5 2.6 collective-permute-start.6
  420.8 3.4 collective-permute-start.7
  442.8 234.0 %all-reduce.20.cloned.1.call-start = ((), (), s32[]{:S(2)}) async-start(), calls=%async_computation.2 | async-start | bytes 1572864 | tf_op jit(solution)/shard_map/psum | solution.py:85
  676.8 62.5 %copy-start.4 = (f32[256,512]{1,0:T(8,128)S(1)}, f32[256,512]{1,0:T(8,128)}, u32[]{:S(2)}) copy-start(f32[256,512]{1,0:T(8,128)} %get-tuple-element.46) | copy-start | bytes 1572868
  677.8 63.9 %copy-start.2 = (f32[256,2048]{1,0:T(8,128)S(1)}, f32[256,2048]{1,0:T(8,128)}, u32[]{:S(2)}) copy-start(f32[256,2048]{1,0:T(8,128)} %all-reduce.18.cloned.1.call-done) | copy-start | bytes 6291460
Sparse Core Ops, SparseCore 0:
  76.9 162.9 all-reduce.15
  243.7 65.6 all-reduce.21
  442.9 163.9 all-reduce.17
  611.1 65.6 all-reduce.19
where the time goes:
time: 763 us; the launch traced here: 755 us
  waiting for transfers between devices  496 us (65%)
  other arithmetic  148 us (19%)
  local copies, waits for them, and re-layouts  59.5 us (8%)
  matrix products  17.7 us (2%)
  starting transfers between devices  17.3 us (2%)
  between operations  16.5 us (2%)
    psum x2, waiting for transfers between devices, shards(): row_panel = lax.psum(row_part, 'row')  318 us
    psum x2, waiting for transfers between devices, shards(): col_panel, innov = lax.psum((col_part, block_part), 'col')  131 us
    another operation x14, other arithmetic, shards(): factor = jnp.linalg.cholesky(innov)  69.2 us
    ppermute x4, waiting for transfers between devices, extended(): lax.ppermute(lax.slice_in_dim(block, 0, width, axis=dim), axis, backward)  41.9 us
    another operation x5, other arithmetic, shards(): gain = jax.scipy.linalg.cho_solve((factor, True), col_panel.T).T  39.6 us
  transfers between devices with their start and end apart: 12, of which 10 were waited for; matrix products, arithmetic and copies ran while one was open for 2% of the time, Pallas kernels for 0%

commit v1 on v0

v1 whole, which is shorter than its diff:
```python
import jax
import jax.numpy as jnp
from jax import lax
from jax.experimental import pallas as pl
from jax.experimental.pallas import tpu as pltpu
from jax.sharding import Mesh, PartitionSpec as P

G = 128
BATCHES = 2
KOBS = 256
HALO = BATCHES * G
ALL = ("z", "y", "x", "k")
COL = ("x", "k")
NB = 128
F32 = jnp.float32


def mm(a, b, dims):
    return lax.dot_general(
        a, b, (dims, ((), ())), precision=lax.Precision.HIGHEST, preferred_element_type=F32
    )


def call(kernel, out_shape, flops, moved, **kw):
    return pl.pallas_call(
        kernel,
        out_shape=out_shape,
        cost_estimate=pl.CostEstimate(flops=flops, bytes_accessed=moved, transcendentals=0),
        **kw,
    )


def lookup(table, line, pos):
    n = line.shape[0]
    lane = lax.broadcasted_iota(jnp.int32, (n, G), 1)
    picked = mm((lane == line).astype(F32), table, ((1,), (0,)))
    hit = lane == pos
    parts = [
        jnp.sum(jnp.where(hit, picked[:, i * G : (i + 1) * G], 0.0), axis=1, keepdims=True)
        for i in range(3)
    ]
    return parts


def spread_taps(table, line, pos):
    a, b, u = lookup(table, line, pos)
    code = u.astype(jnp.int32)
    line2 = line + jnp.where(code % 2 == 1, 1, -1)
    pos2 = pos + jnp.where(code // 2 == 1, 1, -1)
    wl = jnp.where((line2 >= 0) & (line2 < G), a, 0.0)
    wc = jnp.where((pos2 >= 0) & (pos2 < G), b, 0.0)
    return [(line, pos, 1.0 - a - b), (line2, pos, wl), (line, pos2, wc)]


def tap_tile(idx_ref, w_ref, base, width):
    cell = lax.broadcasted_iota(jnp.int32, (KOBS, width), 1) + base
    halves = []
    for half, count in ((0, 3), (1, 9)):
        rows = slice(half * KOBS, (half + 1) * KOBS)
        acc = None
        for m in range(count):
            term = jnp.where(cell == idx_ref[rows, m : m + 1], w_ref[rows, m : m + 1], 0.0)
            acc = term if acc is None else acc + term
        halves.append(acc)
    return jnp.concatenate(halves, axis=0)


def project_kernel(start_ref, obs_ref, table_ref, p_ref, h_ref, idx_ref, w_ref):
    step = pl.program_id(0)
    width = p_ref.shape[1]

    @pl.when(step == 0)
    def _():
        table = table_ref[...]
        obs = obs_ref[...]
        first = spread_taps(table, obs // G, obs % G)
        lane = lax.broadcasted_iota(jnp.int32, (KOBS, 128), 1)
        for half in range(2):
            rows = slice(half * KOBS, (half + 1) * KOBS)
            taps = [(l[rows], p[rows], w[rows]) for l, p, w in first]
            if half == 1:
                taps = [
                    (l2, p2, w * w2)
                    for l, p, w in taps
                    for l2, p2, w2 in spread_taps(table, l, p)
                ]
            idx = jnp.zeros((KOBS, 128), jnp.int32)
            wts = jnp.zeros((KOBS, 128), F32)
            for m, (l, p, w) in enumerate(taps):
                idx = jnp.where(lane == m, l * G + p, idx)
                wts = jnp.where(lane == m, w, wts)
            idx_ref[rows, :] = idx
            w_ref[rows, :] = wts
        h_ref[...] = jnp.zeros_like(h_ref)

    tile = tap_tile(idx_ref, w_ref, start_ref[1] + step * width, width)
    h_ref[...] += mm(tile, p_ref[...], ((1,), (1,)))


def project(starts, obs, table, block):
    rows, cols = block.shape
    n = obs.shape[0]
    width = 256
    return call(
        project_kernel,
        (
            jax.ShapeDtypeStruct((n, rows), F32),
            jax.ShapeDtypeStruct((n, 128), jnp.int32),
            jax.ShapeDtypeStruct((n, 128), F32),
        ),
        2 * n * rows * cols * 6,
        4 * rows * cols,
        grid_spec=pltpu.PrefetchScalarGridSpec(
            num_scalar_prefetch=1,
            grid=(cols // width,),
            in_specs=[
                pl.BlockSpec((n, 1), lambda i, s: (0, 0)),
                pl.BlockSpec(table.shape, lambda i, s: (0, 0)),
                pl.BlockSpec((rows, width), lambda i, s: (0, i)),
            ],
            out_specs=[
                pl.BlockSpec((n, rows), lambda i, s: (0, 0)),
                pl.BlockSpec((n, 128), lambda i, s: (0, 0)),
                pl.BlockSpec((n, 128), lambda i, s: (0, 0)),
            ],
        ),
        name="project",
    )(starts, obs, table, block)


def innov_kernel(start_ref, parts_ref, idx_ref, w_ref, h_ref, t_ref):
    h = parts_ref[0]
    for i in range(1, parts_ref.shape[0]):
        h = h + parts_ref[i]
    h_ref[...] = h
    tile = tap_tile(idx_ref, w_ref, start_ref[0], h.shape[1])
    t_ref[...] = mm(h, tile, ((1,), (1,)))


def innov(starts, parts, idx, w):
    count, some, rows = parts.shape
    n = idx.shape[0]
    vmem = pl.BlockSpec(memory_space=pltpu.VMEM)
    return call(
        innov_kernel,
        (jax.ShapeDtypeStruct((some, rows), F32), jax.ShapeDtypeStruct((some, n), F32)),
        2 * some * rows * n * 6,
        4 * count * some * rows,
        in_specs=[pl.BlockSpec(memory_space=pltpu.SMEM), vmem, vmem, vmem],
        out_specs=[vmem, vmem],
        name="innov",
    )(starts, parts, idx, w)


def stencil(v, coef, axis):
    n = v.shape[axis]
    c, nl, pv, nc, pc = coef
    return (
        c * v
        + nl * pltpu.roll(v, n - G, axis)
        + pv * pltpu.roll(v, G, axis)
        + nc * pltpu.roll(v, n - 1, axis)
        + pc * pltpu.roll(v, 1, axis)
    )


def along_lanes(coef_ref):
    return [coef_ref[i : i + 1, :] for i in range(5)]


def panel_kernel(lo_ref, h_ref, hi_ref, coef_ref, g_ref):
    v = jnp.concatenate([lo_ref[...], h_ref[...], hi_ref[...]], axis=1)
    coef = along_lanes(coef_ref)
    for _ in range(BATCHES):
        v = stencil(v, coef, 1)
    g_ref[...] = v[:, HALO:-HALO]


def panel(lo, h, hi, coef):
    return call(
        panel_kernel, jax.ShapeDtypeStruct(h.shape, F32), 20 * h.size, 16 * h.size, name="panel"
    )(lo, h, hi, coef)


def left_kernel(lo_ref, p_ref, hi_ref, coef_ref, out_ref):
    v = jnp.concatenate([lo_ref[...], p_ref[...], hi_ref[...]], axis=0)
    coef = [coef_ref[:, i : i + 1] for i in range(5)]
    for _ in range(BATCHES):
        v = stencil(v, coef, 0)
    out_ref[...] = v[HALO:-HALO, :]


def left(lo, block, hi, coef):
    rows, cols = block.shape
    width = 256
    spec = lambda r: pl.BlockSpec((r, width), lambda i: (0, i))
    return call(
        left_kernel,
        jax.ShapeDtypeStruct(block.shape, F32),
        40 * block.size,
        12 * block.size,
        grid=(cols // width,),
        in_specs=[spec(HALO), spec(rows), spec(HALO), pl.BlockSpec(coef.shape, lambda i: (0, 0))],
        out_specs=spec(rows),
        name="left",
    )(lo, block, hi, coef)


def final_kernel(lo_ref, l_ref, hi_ref, coef_ref, z_ref, g_ref, out_ref):
    v = jnp.concatenate([lo_ref[...], l_ref[...], hi_ref[...]], axis=1)
    coef = along_lanes(coef_ref)
    for _ in range(BATCHES):
        v = stencil(v, coef, 1)
    out_ref[...] = v[:, HALO:-HALO] - mm(z_ref[...], g_ref[...], ((0,), (0,)))


def final(lo, block, hi, coef, z, g):
    rows, cols = block.shape
    n = z.shape[0]
    height = 128
    spec = lambda c: pl.BlockSpec((height, c), lambda i: (i, 0))
    return call(
        final_kernel,
        jax.ShapeDtypeStruct(block.shape, F32),
        2 * n * rows * cols * 6,
        16 * block.size,
        grid=(rows // height,),
        in_specs=[
            spec(HALO),
            spec(cols),
            spec(HALO),
            pl.BlockSpec(coef.shape, lambda i: (0, 0)),
            pl.BlockSpec((n, height), lambda i: (0, i)),
            pl.BlockSpec(g.shape, lambda i: (0, 0)),
        ],
        out_specs=spec(cols),
        name="final",
    )(lo, block, hi, coef, z, g)


def diag_inverse(block):
    n = block.shape[0]
    tiles = n // 8
    lane = lax.broadcasted_iota(jnp.int32, (8, n), 1)
    sub = lax.broadcasted_iota(jnp.int32, (8, n), 0)
    d = [block[8 * t : 8 * t + 8] for t in range(tiles)]
    b = [(lane == sub + 8 * t).astype(F32) for t in range(tiles)]
    spread = lambda v: jnp.broadcast_to(v, (8, n))
    for p in range(tiles):
        row = [spread(d[p][s : s + 1]) for s in range(8)]
        brow = [spread(b[p][s : s + 1]) for s in range(8)]
        m = [[spread(row[r][:, 8 * p + s : 8 * p + s + 1]) for s in range(r + 1)] for r in range(8)]
        inv, low = [], []
        for s in range(8):
            inv.append(lax.rsqrt(m[s][s]))
            low.append([None] * (s + 1) + [m[r][s] * inv[s] for r in range(s + 1, 8)])
            for r in range(s + 1, 8):
                for q in range(s + 1, r + 1):
                    m[r][q] = m[r][q] - low[s][r] * low[s][q]
            row[s] = row[s] * inv[s]
            brow[s] = brow[s] * inv[s]
            for r in range(s + 1, 8):
                row[r] = row[r] - low[s][r] * row[s]
                brow[r] = brow[r] - low[s][r] * brow[s]
        out = brow[0]
        for s in range(1, 8):
            out = jnp.where(sub == s, brow[s], out)
        b[p] = out
        for s in reversed(range(8)):
            for r in range(s + 1, 8):
                row[s] = row[s] - low[s][r] * row[r]
                brow[s] = brow[s] - low[s][r] * brow[r]
            row[s] = row[s] * inv[s]
            brow[s] = brow[s] * inv[s]
        for t in range(p + 1, tiles):
            raw = d[t]
            for s in range(8):
                col = spread(raw[:, 8 * p + s : 8 * p + s + 1])
                d[t] = d[t] - col * row[s]
                b[t] = b[t] - col * brow[s]
    return jnp.concatenate(b, axis=0)


def factor_kernel(cov_ref, noise_ref, inv_ref, up_ref):
    n = cov_ref.shape[0]
    eye = lax.broadcasted_iota(jnp.int32, (n, n), 0) == lax.broadcasted_iota(jnp.int32, (n, n), 1)
    up_ref[...] = cov_ref[...] + jnp.where(eye, noise_ref[...], 0.0)
    for k in range(n // NB):
        lo, hi = k * NB, (k + 1) * NB
        linv = diag_inverse(up_ref[lo:hi, lo:hi])
        inv_ref[k] = linv
        if hi < n:
            w = mm(linv, up_ref[lo:hi, hi:], ((1,), (0,)))
            up_ref[lo:hi, hi:] = w
            up_ref[hi:, hi:] = up_ref[hi:, hi:] - mm(w, w, ((0,), (0,)))


def factor(cov, noise):
    n = cov.shape[0]
    return call(
        factor_kernel,
        (jax.ShapeDtypeStruct((n // NB, NB, NB), F32), jax.ShapeDtypeStruct((n, n), F32)),
        15 * 10**9,
        8 * cov.size,
        name="factor",
    )(cov, noise)


def solve_kernel(inv_ref, up_ref, g_ref, z_ref):
    blocks = up_ref.shape[0] // NB
    at = lambda i: slice(i * NB, (i + 1) * NB)
    ys = []
    for k in range(blocks):
        acc = g_ref[at(k), :]
        for i in range(k):
            acc = acc - mm(up_ref[at(i), at(k)], ys[i], ((0,), (0,)))
        ys.append(mm(inv_ref[k], acc, ((1,), (0,))))
    zs = [None] * blocks
    for k in reversed(range(blocks)):
        acc = ys[k]
        for i in range(k + 1, blocks):
            acc = acc - mm(up_ref[at(k), at(i)], zs[i], ((1,), (0,)))
        zs[k] = mm(inv_ref[k], acc, ((0,), (0,)))
        z_ref[at(k), :] = zs[k]


def solve(inv, up, g):
    return call(
        solve_kernel, jax.ShapeDtypeStruct(g.shape, F32), 4 * 10**9, 16 * g.size, name="solve"
    )(inv, up, g)


def neighbours(v_low, v_high, axis):
    count = lax.axis_size(axis)
    forward = [(i, i + 1) for i in range(count - 1)]
    backward = [(t, s) for s, t in forward]
    return lax.ppermute(v_high, axis, forward), lax.ppermute(v_low, axis, backward)


def shards(covariance, courant, upwind, observed, noise):
    rows, cols = covariance.shape
    row_start = lax.axis_index(("z", "y")) * rows
    col_start = lax.axis_index(COL) * cols
    starts = jnp.stack([row_start, col_start]).astype(jnp.int32)
    depth, planes = lax.axis_size("z"), lax.axis_size("y")
    across = lax.axis_size(COL)

    top, bottom = neighbours(covariance[:HALO], covariance[-HALO:], ("z", "y"))

    table = jnp.concatenate(
        [courant.reshape(2, G, G), upwind.reshape(1, G, G).astype(F32)], axis=0
    )
    table = table.transpose(1, 0, 2).reshape(G, 3 * G)
    obs = observed.reshape(-1, 1)
    partial, idx, w = project(starts, obs, table, covariance)
    some = partial.shape[0] // across
    parts = lax.all_to_all(partial.reshape(across, some, rows), COL, 0, 0, tiled=True)
    h, t = innov(starts, parts, idx, w)

    t = lax.all_to_all(t.reshape(depth, some // depth, -1), "z", 0, 0, tiled=True).sum(0)
    t = lax.all_gather(t, "y", axis=0).sum(0)
    t = lax.all_gather(t, "z", axis=0, tiled=True)
    t = lax.all_to_all(jnp.broadcast_to(t[None], (across,) + t.shape), COL, 0, 0, tiled=True)
    cov = t.reshape(BATCHES * KOBS, BATCHES * KOBS)

    a, b = courant[0], courant[1]
    line_up, cell_up = upwind % 2 == 1, upwind // 2 == 1
    pos = jnp.arange(a.shape[0]) % G
    coef = jnp.stack(
        [
            1.0 - a - b,
            jnp.where(line_up, a, 0.0),
            jnp.where(line_up, 0.0, a),
            jnp.where(cell_up & (pos < G - 1), b, 0.0),
            jnp.where(cell_up | (pos == 0), 0.0, b),
        ]
    )
    coef = jnp.pad(coef, ((0, 3), (HALO, HALO)))
    row_coef = lax.dynamic_slice_in_dim(coef, row_start, rows + 2 * HALO, 1)
    col_coef = lax.dynamic_slice_in_dim(coef, col_start, cols + 2 * HALO, 1)

    before, after = neighbours(h[:, :HALO], h[:, -HALO:], ("z", "y"))
    g = panel(before, h, after, row_coef)
    g_rows = lax.all_gather(g, COL, axis=0, tiled=True)
    turn = [
        ((z * planes + y) * across + c, (c * planes + y) * across + z)
        for z in range(depth)
        for y in range(planes)
        for c in range(across)
    ]
    g_cols = lax.ppermute(g, ALL, turn)
    g_cols = lax.all_gather(g_cols, "y", axis=1, tiled=True)
    g_cols = lax.all_gather(g_cols, "z", axis=0, tiled=True)

    top, bottom, cov = lax.optimization_barrier((top, bottom, cov))
    moved = left(top, covariance, bottom, row_coef.T)
    before, after = neighbours(moved[:, :HALO], moved[:, -HALO:], COL)
    inv, up = factor(cov, noise.reshape(1, -1))
    z = solve(inv, up, g_rows)
    return final(before, moved, after, col_coef, z, g_cols)


def solution(mesh):
    fine = Mesh(mesh.devices.reshape(8, 4, 4, 2), ALL)
    spec = P(("z", "y"), COL)
    return jax.shard_map(
        shards, mesh=fine, in_specs=(spec, P(), P(), P(), P()), out_specs=spec, check_vma=False
    )
```

time: 763 us -> 343 us (0.45)
  waiting for transfers between devices: 496 us -> 32 us
  blocking collectives: 0 us -> 154 us
  other arithmetic: 148 us -> 1.69 us
  Pallas kernels: 0 us -> 91.8 us
  local copies, waits for them, and re-layouts: 59.5 us -> 18.7 us
  matrix products: 17.7 us -> 0 us
    psum x4 -> x0, waiting for transfers between devices: 450 us -> none  [the longest x2 318 us: shards(): row_panel = lax.psum(row_part, 'row')]
    all_gather x0 -> x3, blocking collectives: none -> 125 us  [the longest x1 82.3 us: shards(): t = lax.all_gather(t, 'y', axis=0).sum(0)]
    another operation x19 -> x1, other arithmetic: 109 us -> 0.58 us  [shards(): starts = jnp.stack([row_start, col_start]).astype(jnp.int32)]
    pallas_call x0 -> x7, Pallas kernels: none -> 91.8 us  [the longest x1 26.3 us: factor(): call(factor_kernel, (jax.ShapeDtypeStruct((n // NB, NB, NB), F32), jax.Sh...]
    ppermute x8 -> x7, waiting for transfers between devices: 46 us -> 3.18 us  [the longest x3 3.17 us: neighbours(): lax.ppermute(v_low, axis, backward)]
    all_to_all x0 -> x1, blocking collectives: none -> 29.8 us  [shards(): lax.all_to_all(t.reshape(depth, some // depth, -1), 'z', 0, 0, tiled=True)]
    all_to_all x0 -> x2, waiting for transfers between devices: none -> 28.8 us  [the longest x1 15.1 us: shards(): lax.all_to_all(partial.reshape(across, some, rows), COL, 0, 0, tiled=True)]
    reshape x4 -> x1, local copies, waits for them, and re-layouts: 21.5 us -> 0.82 us  [shards(): table = table.transpose(1, 0, 2).reshape(G, 3 * G)]
  transfers between devices with their start and end apart: 12 -> 11, of which waited for: 10 -> 3; matrix products, arithmetic and copies ran while one was open for 2% -> 3% of each run, Pallas kernels for 0% -> 14%
where the time goes in v1:
time: 343 us; the launch traced here: 337 us
  blocking collectives  154 us (45%)
  Pallas kernels  91.8 us (27%)
  waiting for transfers between devices  32 us (9%)
  starting transfers between devices  24.9 us (7%)
  local copies, waits for them, and re-layouts  18.7 us (5%)
  between operations  13.6 us (4%)
    all_gather x1, blocking collectives, shards(): t = lax.all_gather(t, 'y', axis=0).sum(0)  82.3 us
    all_to_all x1, blocking collectives, shards(): lax.all_to_all(t.reshape(depth, some // depth, -1), 'z', 0, 0, tiled=True)  29.8 us
    pallas_call x1, Pallas kernels, factor(): call(factor_kernel, (jax.ShapeDtypeStruct((n // NB, NB, NB), F32), jax.Sh...  26.3 us
    all_gather x1, blocking collectives, shards(): t = lax.all_gather(t, 'z', axis=0, tiled=True)  26 us
    pallas_call x1, Pallas kernels, project(): call(project_kernel, (jax.ShapeDtypeStruct((n, rows), F32), jax.ShapeDtyp...  22.4 us
    pallas_call x1, Pallas kernels, final(): call(final_kernel, jax.ShapeDtypeStruct(block.shape, F32), 2 * n * rows *...  16.4 us
    all_gather x1, blocking collectives, shards(): g_cols = lax.all_gather(g_cols, 'y', axis=1, tiled=True)  16.3 us
    all_to_all x1, waiting for transfers between devices, shards(): lax.all_to_all(partial.reshape(across, some, rows), COL, 0, 0, tiled=True)  15.1 us
  transfers between devices with their start and end apart: 11, of which 3 were waited for; matrix products, arithmetic and copies ran while one was open for 3% of the time, Pallas kernels for 14%

profile of v1, /device:TPU:8, one launch (start us, length us, event | category | flops | bytes accessed | tf_op | source)
XLA Modules:
  0.0 337.2 jit_solution(11472219360884288935)
XLA Ops:
  6.5 0.9 copy.24
  10.0 0.9 copy.20
  11.4 22.4 %project.1 = (f32[512,512]{1,0:T(8,128)}, s32[512,128]{1,0:T(8,128)}, f32[512,128]{1,0:T(8,128)}) custom-call(s32[2]{0:T(128)} %pad_add_fusion.start_ref, s32[512,1]{1,0:T(8,128)} %bitcast.37, f32[128,384]{1,0:T(8,128)} %copy.17.table_ref, f32[512,2048]{1,0:T(8,128)} %p_ref.3), custom_call_target="tpu_custom_call" | custom-call | flops 6442450944 | bytes 4194304 | tf_op jit(solution)/shard_map/project/pallas_call | solution.py:104
  33.8 4.3 %all-to-all-start = ((f32[8,64,512]{2,1,0:T(8,128)}), f32[8,64,512]{2,1,0:T(8,128)S(1)}, u32[]{:S(2)}, u32[]{:S(2)}) async-start(f32[8,64,512]{2,1,0:T(8,128)} %bitcast.31), calls=%async_computation | async-start | bytes 2097152 | tf_op jit(solution)/shard_map/all_to_all | solution.py:357
  39.0 15.1 %all-to-all-done.parts_ref = f32[8,64,512]{2,1,0:T(8,128)S(1)} async-done(((f32[8,64,512]{2,1,0:T(8,128)}), f32[8,64,512]{2,1,0:T(8,128)S(1)}, u32[]{:S(2)}, u32[]{:S(2)}) %all-to-all-start) | async-done | bytes 1048608 | tf_op jit(solution)/shard_map/all_to_all | solution.py:357
  54.0 1.0 copy-done
  55.0 4.2 %innov.1 = (f32[64,512]{1,0:T(8,128)}, f32[64,512]{1,0:T(8,128)}) custom-call(s32[2]{0:T(128)} %pad_add_fusion.start_ref, f32[8,64,512]{2,1,0:T(8,128)} %copy-done, s32[512,128]{1,0:T(8,128)} %get-tuple-element.16.idx_ref, f32[512,128]{1,0:T(8,128)} %get-tuple-element.17.w_ref), custom_call_target="tpu_custom_call" | custom-call | flops 201326592 | bytes 1048576 | tf_op jit(solution)/shard_map/innov/pallas_call | solution.py:144
  59.2 0.9 fusion.15
  60.0 3.5 %collective-permute-start.4 = (f32[64,256]{1,0:T(8,128)S(1)}, f32[64,256]{1,0:T(8,128)S(1)}, u32[]{:S(2)}, u32[]{:S(2)}) collective-permute-start(f32[64,256]{1,0:T(8,128)S(1)} %get-tuple-element.30), channel_id=1, source_target_pairs={{0,8},{8,16},{16,24},{24,32},{32,40},{40,48},{48,56},{56,64},{64,7... | collective-permute-start | bytes 196616 | tf_op jit(solution)/shard_map/ppermute | solution.py:337
  63.5 2.4 collective-permute-start.5
  66.5 3.2 collective-permute-done.5.hi_ref
  70.3 1.9 panel.1
  72.3 1.6 collective-permute-start.6
  73.8 16.3 %all_gather.22 = f32[64,2048]{1,0:T(8,128)} all-gather(f32[64,512]{1,0:T(8,128)S(1)} %collective-permute-done.6), channel_id=1, replica_groups=mesh['z'=8,'y'=4,'x'=4,'k'=2] {'y'}, dimensions={1}, use_global_device_ids=true | all-gather | bytes 655360 | tf_op jit(solution)/shard_map/all_gather | solution.py:392
  90.2 4.8 %fusion.14 = (f32[256,2048]{1,0:T(8,128)}, f32[256,2048]{1,0:T(8,128)}) fusion(f32[512,2048]{1,0:T(8,128)} %p_ref.3), kind=kLoop, calls=%fused_computation.32 | loop fusion | bytes 8388608 | tf_op jit(solution)/shard_map/slice | solution.py:348
  95.0 1.9 collective-permute-start
  96.9 4.1 %collective-permute-start.1 = (f32[256,2048]{1,0:T(8,128)}, f32[256,2048]{1,0:T(8,128)}, u32[]{:S(2)}, u32[]{:S(2)}) collective-permute-start(f32[256,2048]{1,0:T(8,128)} %get-tuple-element.27), channel_id=1, source_target_pairs={{8,0},{16,8},{24,16},{32,24},{40,32},{48,40},{56,48},{64,56},{72,6... | collective-permute-start | bytes 6291464 | tf_op jit(solution)/shard_map/ppermute | solution.py:337
  101.0 29.8 %all_to_all.15 = f32[8,8,512]{2,1,0:T(8,128)S(1)} all-to-all(f32[8,8,512]{2,1,0:T(8,128)S(1)} %bitcast.42), channel_id=1, replica_groups=mesh['z'=8,'y'=4,'x'=4,'k'=2] {'z'}, dimensions={0} | all-to-all | bytes 262144 | tf_op jit(solution)/shard_map/all_to_all | solution.py:360
  130.8 82.3 %all-gather = f32[32,512]{1,0:T(8,128)S(1)} all-gather(f32[8,512]{1,0:T(8,128)S(1)} %reduce_sum.18), channel_id=2, replica_groups=mesh['z'=8,'y'=4,'x'=4,'k'=2] {'y'}, dimensions={0}, use_global_device_ids=true | all-gather | bytes 81920 | tf_op jit(solution)/shard_map/all_gather | solution.py:361
  213.1 26.0 %all_gather.20 = f32[64,512]{1,0:T(8,128)S(1)} all-gather(f32[8,512]{1,0:T(8,128)S(1)} %bitcast_reduce_fusion), channel_id=1, replica_groups=mesh['z'=8,'y'=4,'x'=4,'k'=2] {'z'}, dimensions={0}, use_global_device_ids=true | all-gather | bytes 147456 | tf_op jit(solution)/shard_map/all_gather | solution.py:362
  239.1 1.1 broadcast_in_dim.14
  240.2 4.2 %all-to-all-start.2 = ((f32[8,64,512]{2,1,0:T(8,128)}), f32[8,64,512]{2,1,0:T(8,128)}, u32[]{:S(2)}, u32[]{:S(2)}) async-start(f32[8,64,512]{2,1,0:T(8,128)} %broadcast_in_dim.14), calls=%async_computation.2 | async-start | bytes 2097152 | tf_op jit(solution)/shard_map/all_to_all | solution.py:363
  245.0 1.0 copy.18.coef_ref
  246.7 13.7 %all-to-all-done.2 = f32[8,64,512]{2,1,0:T(8,128)} async-done(((f32[8,64,512]{2,1,0:T(8,128)}), f32[8,64,512]{2,1,0:T(8,128)}, u32[]{:S(2)}, u32[]{:S(2)}) %all-to-all-start.2) | async-done | bytes 1048608 | tf_op jit(solution)/shard_map/all_to_all | solution.py:363
  260.4 1.3 copy-done.1
  261.7 12.0 %left.1.l_ref = f32[512,2048]{1,0:T(8,128)} custom-call(f32[256,2048]{1,0:T(8,128)} %copy-done.1, f32[512,2048]{1,0:T(8,128)} %p_ref.3, f32[256,2048]{1,0:T(8,128)} %collective-permute-done.1.hi_ref, f32[1024,8]{1,0:T(8,128)} %copy.18.coef_ref), custom_call_target="tpu_custom_call" | custom-call | flops 41943040 | bytes 12582912 | tf_op jit(solution)/shard_map/left/pallas_call | solution.py:197
  273.7 1.3 fusion.13
  275.0 1.5 collective-permute-start.2
  276.5 1.5 collective-permute-start.3
  278.0 26.3 %factor.1 = (f32[4,128,128]{2,1,0:T(8,128)}, f32[512,512]{1,0:T(8,128)}) custom-call(f32[512,512]{1,0:T(8,128)} %bitcast.8.cov_ref, f32[1,512]{1,0:T(1,128)} %bitcast.46), custom_call_target="tpu_custom_call" | custom-call | flops 15000000512 | bytes 2097152 | tf_op jit(solution)/shard_map/factor/pallas_call | solution.py:300
  304.3 8.6 %solve.1.z_ref = f32[512,512]{1,0:T(8,128)} custom-call(f32[4,128,128]{2,1,0:T(8,128)} %get-tuple-element.22.inv_ref, f32[512,512]{1,0:T(8,128)} %get-tuple-element.23.up_ref, f32[512,512]{1,0:T(8,128)} %all-gather.4.cloned.1.call-done.g_ref), custom_call_target="tpu_custom_call" | custom-call | flops 4000000000 | bytes 4194304 | tf_op jit(solution)/shard_map/solve/pallas_call | solution.py:328
  313.9 16.4 %final.1 = f32[512,2048]{1,0:T(8,128)} custom-call(f32[512,256]{1,0:T(8,128)} %copy-done.8, f32[512,2048]{1,0:T(8,128)} %left.1.l_ref, f32[512,256]{1,0:T(8,128)} %copy-done.9, f32[8,2560]{1,0:T(8,128)} %pad_dynamic-slice_fusion.coef_ref, f32[512,512]{1,0:T(8,128)} %solve.1.z_ref, f32[512,2048]{1,0:T(8,128)} %all-gather.6.cloned.1.call-done.g_ref), custom_call_target="tpu_custom_call" | custom-call | flops 6442450944 | bytes 16777216 | tf_op jit(solution)/shard_map/final/pallas_call | solution.py:222
  (45 shorter events, 7.4 us)
Async XLA Ops:
  11.4 26.8 %copy-start.2 = (f32[2,16384]{1,0:T(2,128)S(1)}, f32[2,16384]{1,0:T(2,128)}, u32[]{:S(2)}) copy-start(f32[2,16384]{1,0:T(2,128)} %param.6) | copy-start | bytes 393220
  11.4 26.9 %copy-start.3 = (s32[16384]{0:T(1024)S(1)}, s32[16384]{0:T(1024)}, u32[]{:S(2)}) copy-start(s32[16384]{0:T(1024)} %param.7) | copy-start | bytes 196612
  33.8 20.2 %all-to-all-start = ((f32[8,64,512]{2,1,0:T(8,128)}), f32[8,64,512]{2,1,0:T(8,128)S(1)}, u32[]{:S(2)}, u32[]{:S(2)}) async-start(f32[8,64,512]{2,1,0:T(8,128)} %bitcast.31), calls=%async_computation | async-start | bytes 2097152 | tf_op jit(solution)/shard_map/all_to_all | solution.py:357
  38.1 266.2 %all-gather.4.cloned.1.call-start = ((), (), s32[]{:S(2)}) async-start(), calls=%async_computation.3 | async-start | bytes 1179648 | tf_op jit(solution)/shard_map/all_gather | solution.py:384
  54.0 1.0 copy-start
  60.0 6.5 %collective-permute-start.4 = (f32[64,256]{1,0:T(8,128)S(1)}, f32[64,256]{1,0:T(8,128)S(1)}, u32[]{:S(2)}, u32[]{:S(2)}) collective-permute-start(f32[64,256]{1,0:T(8,128)S(1)} %get-tuple-element.30), channel_id=1, source_target_pairs={{0,8},{8,16},{16,24},{24,32},{32,40},{40,48},{48,56},{56,64},{64,7... | collective-permute-start | bytes 196616 | tf_op jit(solution)/shard_map/ppermute | solution.py:337
  63.5 6.2 %collective-permute-start.5 = (f32[64,256]{1,0:T(8,128)S(1)}, f32[64,256]{1,0:T(8,128)S(1)}, u32[]{:S(2)}, u32[]{:S(2)}) collective-permute-start(f32[64,256]{1,0:T(8,128)S(1)} %get-tuple-element.29), channel_id=1, source_target_pairs={{8,0},{16,8},{24,16},{32,24},{40,32},{48,40},{56,48},{64,56},{72,6... | collective-permute-start | bytes 196616 | tf_op jit(solution)/shard_map/ppermute | solution.py:337
  66.5 3.2 copy-start.5
  69.7 0.6 copy-start.6
  72.2 240.7 %all-gather.6.cloned.1.call-start = ((), (), s32[]{:S(2)}) async-start(), calls=%async_computation.4 | async-start | bytes 4718592 | tf_op jit(solution)/shard_map/all_gather | solution.py:393
  72.3 1.6 collective-permute-start.6
  90.1 10.8 %copy-start.4 = (f32[64,512]{1,0:T(8,128)S(1)}, f32[64,512]{1,0:T(8,128)}, u32[]{:S(2)}) copy-start(f32[64,512]{1,0:T(8,128)} %get-tuple-element.18) | copy-start | bytes 393220
  90.2 154.3 %copy-start.7 = (f32[2,256]{1,0:T(2,128)S(1)}, f32[2,256]{1,0:T(2,128)}, u32[]{:S(2)}) copy-start(f32[2,256]{1,0:T(2,128)} %param.9) | copy-start | bytes 6148
  95.0 165.4 %collective-permute-start = (f32[256,2048]{1,0:T(8,128)}, f32[256,2048]{1,0:T(8,128)S(1)}, u32[]{:S(2)}, u32[]{:S(2)}) collective-permute-start(f32[256,2048]{1,0:T(8,128)} %get-tuple-element.28), channel_id=1, source_target_pairs={{0,8},{8,16},{16,24},{24,32},{32,40},{40,48},{48,56},{56,64},{64,7... | collective-permute-start | bytes 6291464 | tf_op jit(solution)/shard_map/ppermute | solution.py:337
  96.9 163.5 %collective-permute-start.1 = (f32[256,2048]{1,0:T(8,128)}, f32[256,2048]{1,0:T(8,128)}, u32[]{:S(2)}, u32[]{:S(2)}) collective-permute-start(f32[256,2048]{1,0:T(8,128)} %get-tuple-element.27), channel_id=1, source_target_pairs={{8,0},{16,8},{24,16},{32,24},{40,32},{48,40},{56,48},{64,56},{72,6... | collective-permute-start | bytes 6291464 | tf_op jit(solution)/shard_map/ppermute | solution.py:337
  240.2 20.2 %all-to-all-start.2 = ((f32[8,64,512]{2,1,0:T(8,128)}), f32[8,64,512]{2,1,0:T(8,128)}, u32[]{:S(2)}, u32[]{:S(2)}) async-start(f32[8,64,512]{2,1,0:T(8,128)} %broadcast_in_dim.14), calls=%async_computation.2 | async-start | bytes 2097152 | tf_op jit(solution)/shard_map/all_to_all | solution.py:363
  260.4 1.3 copy-start.1
  275.0 37.9 %collective-permute-start.2 = (f32[512,256]{1,0:T(8,128)S(1)}, f32[512,256]{1,0:T(8,128)S(1)}, u32[]{:S(2)}, u32[]{:S(2)}) collective-permute-start(f32[512,256]{1,0:T(8,128)S(1)} %get-tuple-element.26), channel_id=1, source_target_pairs={{0,1},{1,2},{2,3},{3,4},{4,5},{5,6},{6,7},{8,9},{9,10},{10,11},{11... | collective-permute-start | bytes 1572872 | tf_op jit(solution)/shard_map/ppermute | solution.py:337
  276.5 36.4 %collective-permute-start.3 = (f32[512,256]{1,0:T(8,128)S(1)}, f32[512,256]{1,0:T(8,128)S(1)}, u32[]{:S(2)}, u32[]{:S(2)}) collective-permute-start(f32[512,256]{1,0:T(8,128)S(1)} %get-tuple-element.25), channel_id=1, source_target_pairs={{1,0},{2,1},{3,2},{4,3},{5,4},{6,5},{7,6},{9,8},{10,9},{11,10},{12... | collective-permute-start | bytes 1572872 | tf_op jit(solution)/shard_map/ppermute | solution.py:337
  312.9 0.8 copy-start.8
  312.9 1.0 copy-start.9
Sparse Core Ops, SparseCore 0:
  72.3 28.5 all-gather.3
  102.7 57.4 all-gather.5
